TPU v7x, 32 devices: a whole 2x2x4 slice. The times are simulated.
32 devices in a mesh: gx: 4 (over y, x), gy: 8 (over z, core).
Axes of the slice: x: 2, y: 2, z: 4, core: 2. Of those that a mesh axis runs over, the one named last changes fastest.
Arguments:
- velocity: float32 [3, 32, 128, 256], P(None, 'gx', 'gy'), may hold values from -6 to 6
- pressure: float32 [32, 128, 256], P('gx', 'gy'), may hold values from -4 to 4
- part_cell: int32 [4, 8, 8, 512], P('gx', 'gy'), may hold values from 0 to 32767
- part_count: int32 [4, 8, 8], P('gx', 'gy'), may hold values from 1 to 512, as said below
- grain_velocities: float32 [4, 8, 8, 3, 512], P('gx', 'gy'), may hold values from -6 to 6
- part_vol: float32 [4, 8, 8, 512], P('gx', 'gy'), may hold values from 0.05 to 0.3
Outputs:
- velocity_out: float32 [3, 32, 128, 256], P(None, 'gx', 'gy')
- pressure_out: float32 [32, 128, 256], P('gx', 'gy')
- drag: float32 [4, 8, 8, 3, 512], P('gx', 'gy')
Inputs may be any that keep to these rules, and one draw needn't show every extreme that they name: Every DEM owner (a, b) has at least one c with part_count[a, b, c] equal to 512.
All inputs are finite; a program needn't handle non-finite values.
Results may differ from a plain program's by a relative error of at most 0.00002.
Values sent between devices are 32-bit elements; how exact they have to be, the bound alone decides.
A program may use at most 128 MiB of HBM per device.

v0:
```python
import jax
import jax.numpy as jnp
from jax import lax
from jax.experimental import pallas as pl
from jax.experimental.pallas import tpu as pltpu
from jax.sharding import PartitionSpec as P

STEPS = 2
SWEEPS = 4
DRAG = 2.0
DT = 0.25
VISC = 0.2
FLOOR = 0.4

WX = SWEEPS + 1
WY = 8
ROWS = 8

MESH = pl.DeviceIdType.MESH
CORNERS = ((0, 0), (0, 1), (1, 0), (1, 1))
F32 = jnp.float32
BF16 = jnp.bfloat16


def split(value):
    high = value.astype(BF16).astype(F32)
    return high, value - high


def body(n_gx, n_gy, count_ref, vel_ref, p_ref, cell_ref, gv_ref, vol_ref,
         vel_out, p_out, drag_out,
         v1, v2, pin1, pin2, pa, pb, src1, src2, sp, solid, mf, eps, coef, rate, pull,
         guess, flux, dep, pk, rk, dk, rd, ft, corner_out, corner_in, field_send, field_recv, part_send, part_recv):
    bx, by, nz = p_ref.shape
    ex, ey = bx + 2 * WX, by + 2 * WY
    slots = vol_ref.shape[-1]
    columns = bx * by
    ix, iy = lax.axis_index("gx"), lax.axis_index("gy")
    has = {("x", 0): ix > 0, ("x", 1): ix < n_gx - 1, ("y", 0): iy > 0, ("y", 1): iy < n_gy - 1}
    peer = {("x", 0): (ix - 1, iy), ("x", 1): (ix + 1, iy), ("y", 0): (ix, iy - 1), ("y", 1): (ix, iy + 1)}
    own_x, own_y = pl.ds(WX, bx), pl.ds(WY, by)

    def beyond(corner):
        return ix + (2 * corner[0] - 1), iy + (2 * corner[1] - 1)

    barrier = pltpu.get_barrier_semaphore()
    for k in range(1, n_gy):
        pl.semaphore_signal(barrier, inc=1, device_id=(ix, lax.rem(iy + k, n_gy)), device_id_type=MESH)
    for side in (0, 1):
        @pl.when(has["x", side])
        def _():
            pl.semaphore_signal(barrier, inc=1, device_id=peer["x", side], device_id_type=MESH)
    for corner in CORNERS:
        @pl.when(has["x", corner[0]] & has["y", corner[1]])
        def _():
            pl.semaphore_signal(barrier, inc=1, device_id=beyond(corner), device_id_type=MESH)

    slot = lax.broadcasted_iota(jnp.int32, (1, slots), 1)
    for c in range(n_gy):
        cell = cell_ref[pl.ds(c, 1), :]
        column = lax.div(cell, nz)
        pk[c, 0:1, :] = column.astype(F32)
        pk[c, 1:2, :] = (cell - column * nz).astype(F32)
        pk[c, 2:3, :] = jnp.where(slot < count_ref[c], vol_ref[pl.ds(c, 1), :], 0.0)
        for d in range(3):
            pk[c, 3 + d:4 + d, :] = gv_ref[d, pl.ds(c, 1), :]
        pk[c, 6:8, :] = jnp.zeros((2, slots), F32)

    fields = [v1.at[d] for d in range(3)] + [v2.at[d] for d in range(3)] + [mf.at[d] for d in range(3)]
    fields += [pin1, pin2, src1, src2, solid]
    for side in (0, 1):
        @pl.when(jnp.logical_not(has["x", side]))
        def _():
            for field in fields:
                at = 0 if side == 0 else WX + bx
                field[pl.ds(at, WX)] = jnp.zeros((WX, ey, nz), F32)

        @pl.when(jnp.logical_not(has["y", side]))
        def _():
            for field in fields:
                at = 0 if side == 0 else WY + by
                field[:, pl.ds(at, WY), :] = jnp.zeros((ex, WY, nz), F32)

    x_peers = jnp.where(ix > 0, 1, 0) + jnp.where(ix < n_gx - 1, 1, 0)
    y_peers = jnp.where(iy > 0, 1, 0) + jnp.where(iy < n_gy - 1, 1, 0)
    pl.semaphore_wait(barrier, n_gy - 1 + x_peers * (1 + y_peers))

    def particles(k, source, landing, bank):
        return pltpu.make_async_remote_copy(
            src_ref=source, dst_ref=landing, send_sem=part_send.at[bank, k], recv_sem=part_recv.at[bank, k],
            device_id=(ix, lax.rem(iy + k, n_gy)), device_id_type=MESH)

    def outgoing(k):
        return particles(k, pk.at[lax.rem(iy + k, n_gy)], rk.at[iy], 0)

    def incoming(k):
        return particles(k, pk.at[0], rk.at[lax.rem(iy + n_gy - k, n_gy)], 0)

    for k in range(1, n_gy):
        outgoing(k).start()
    rk[iy] = pk[iy]

    class Halo:
        def __init__(self, slot, ref, width, reach=0, own=None, axes="xy", skip=0):
            self.slot, self.ref, self.width, self.own, self.axes, self.skip = slot, ref, width, own, axes, skip
            self.rows = [(i, j) for i in range(reach) for j in range(reach) if i + j + 2 <= reach]

        def copy(self, index, source, landing, to):
            return pltpu.make_async_remote_copy(
                src_ref=source, dst_ref=landing, send_sem=field_send.at[self.slot, index],
                recv_sem=field_recv.at[self.slot, index], device_id=to, device_id_type=MESH)

        def x_copy(self, side):
            w, skip = self.width, self.skip
            at = skip if side == 0 else bx - w - skip
            if self.own is None:
                source = self.ref.at[pl.ds(WX + at, w), own_y]
            else:
                source = self.own.at[pl.ds(at, w)]
            landing = self.ref.at[pl.ds(WX + bx + skip if side == 0 else WX - w - skip, w), own_y]
            return self.copy(side, source, landing, peer["x", side])

        def y_copy(self, side):
            at = 0 if side == 0 else by - WY
            if self.own is None:
                source = self.ref.at[own_x, pl.ds(WY + at, WY)]
            else:
                source = self.own.at[:, pl.ds(at, WY)]
            landing = self.ref.at[own_x, pl.ds(WY + by if side == 0 else 0, WY)]
            return self.copy(2 + side, source, landing, peer["y", side])

        def c_copy(self, corner):
            n = 2 * corner[0] + corner[1]
            size = -(-len(self.rows) // 8) * 8
            return self.copy(4 + n, corner_out.at[self.slot, n, pl.ds(0, size)],
                             corner_in.at[self.slot, n, pl.ds(0, size)], beyond(corner))

        def pack(self):
            for corner in CORNERS if self.rows else ():
                for n, (i, j) in enumerate(self.rows):
                    x = WX + (i if corner[0] == 0 else bx - 1 - i)
                    y = WY + (j if corner[1] == 0 else by - 1 - j)
                    corner_out[self.slot, 2 * corner[0] + corner[1], n:n + 1, :] = self.ref[x, y:y + 1, :]

        def each(self, axis, act, flip=False):
            if axis == "c":
                for corner in CORNERS if self.rows else ():
                    near = (1 - corner[0], 1 - corner[1]) if flip else corner

                    @pl.when(has["x", near[0]] & has["y", near[1]])
                    def _():
                        act(self.c_copy(corner), corner)
            elif axis in self.axes:
                for side in (0, 1):
                    @pl.when(has[axis, 1 - side if flip else side])
                    def _():
                        act((self.x_copy if axis == "x" else self.y_copy)(side), None)

        def unpack(self, copy, corner):
            copy.wait_recv()
            for n, (i, j) in enumerate(self.rows):
                x = WX + bx + i if corner[0] == 0 else WX - 1 - i
                y = WY + by + j if corner[1] == 0 else WY - 1 - j
                self.ref[x, y:y + 1, :] = corner_in[self.slot, 2 * corner[0] + corner[1], n:n + 1, :]

    sent = []

    def start(halos):
        for h in halos:
            h.pack()
        for axis in "cxy":
            for h in halos:
                h.each(axis, lambda c, _: c.start())
        sent.extend(halos)

    def arrive(halos):
        for h in halos:
            h.each("y", lambda c, _: c.wait_recv(), flip=True)
            h.each("x", lambda c, _: c.wait_recv(), flip=True)
        for h in halos:
            h.each("c", h.unpack, flip=True)

    h_vel = [[Halo(0, v1.at[0], 2, 2, vel_ref.at[0]), Halo(1, v1.at[1], 1, 2, vel_ref.at[1]), Halo(2, v1.at[2], 1, 0, vel_ref.at[2])],
             [Halo(3, v2.at[0], 2, 2), Halo(4, v2.at[1], 1, 2), Halo(5, v2.at[2], 1)]]
    h_p = [[Halo(6, pin1, WX, WX, p_ref)], [Halo(7, pin2, WX, WX)]]
    h_src = [[Halo(8, src1, SWEEPS, SWEEPS)], [Halo(9, src2, SWEEPS, SWEEPS)]]
    h_solid = [Halo(10, solid, 2, WX)]
    h_rest = [Halo(13, solid, WX - 2, axes="x", skip=2)]
    h_mf = [Halo(11, mf.at[0], 1, axes="x"), Halo(12, mf.at[1], 1, axes="y")]

    for d in range(3):
        v1[d, own_x, own_y, :] = vel_ref[d]
    pin1[own_x, own_y, :] = p_ref[...]
    start(h_vel[0] + h_p[0])

    column_of = lax.broadcasted_iota(jnp.int32, (columns, slots), 0).astype(F32)
    depth_of = lax.broadcasted_iota(jnp.int32, (nz, slots), 0).astype(F32)
    dep[...] = jnp.zeros_like(dep)
    def deposit(b, carry):
        hot_c = rk[b, 0:1, :] == column_of
        hot_z = jnp.where(rk[b, 1:2, :] == depth_of, 1.0, 0.0).astype(BF16)
        volume = rk[b, 2:3, :]
        values = [volume] + [volume * rk[b, 3 + d:4 + d, :] for d in range(3)]
        parts = [split(value) for value in values]
        both = None
        for side in (0, 1):
            left = jnp.concatenate([jnp.where(hot_c, part[side], 0.0).astype(BF16) for part in parts], axis=0)
            term = lax.dot_general(left, hot_z, (((1,), (1,)), ((), ())), preferred_element_type=F32)
            both = term if both is None else both + term
        dep[...] += both
        return carry

    deposit(iy, 0)

    def deposit_from(k, carry):
        incoming(k).wait_recv()
        return deposit(lax.rem(iy + n_gy - k, n_gy), carry)

    lax.fori_loop(1, n_gy, deposit_from, 0)
    solid[own_x, own_y, :] = dep[pl.ds(0, columns), :].reshape(bx, by, nz)
    for d in range(3):
        mf[d, own_x, own_y, :] = dep[pl.ds((1 + d) * columns, columns), :].reshape(bx, by, nz)
    start(h_solid + h_mf)
    start(h_rest)
    arrive(h_solid + h_mf)
    arrive(h_vel[0])

    row = lax.broadcasted_iota(jnp.int32, (ey, nz), 0)
    depth = lax.broadcasted_iota(jnp.int32, (ey, nz), 1)
    row_in = jnp.where((row >= WY) | (iy > 0), 1.0, 0.0) * jnp.where((row < WY + by) | (iy < n_gy - 1), 1.0, 0.0)

    def voidage(x, carry):
        x_in = ((x >= WX) | (ix > 0)) & ((x < WX + bx) | (ix < n_gx - 1))
        eps[x] = jnp.maximum(1.0 - solid[x], FLOOR) * (row_in * jnp.where(x_in, 1.0, 0.0))
        return carry

    lax.fori_loop(WX - 2, WX + bx + 2, voidage, 0, unroll=4)

    def up_y(v):
        return pltpu.roll(v, ey - 1, 0)

    def down_y(v):
        return pltpu.roll(v, 1, 0)

    def up_z(v):
        return pltpu.roll(v, nz - 1, 1)

    def down_z(v):
        return pltpu.roll(v, 1, 1)

    last_z, first_z = depth == nz - 1, depth == 0

    def weights(x, carry):
        e = eps[x]
        near = [eps[x + 1], eps[x - 1], up_y(e), down_y(e),
                jnp.where(last_z, 0.0, up_z(e)), jnp.where(first_z, 0.0, down_z(e))]
        total = 0.5 * (6.0 * e + (((near[0] + near[1]) + (near[2] + near[3])) + (near[4] + near[5])))
        inside = e > 0.0
        inverse = jnp.where(inside, 0.5 / jnp.where(inside, total, 1.0), 0.0)
        for n in range(6):
            w = (e + near[n]) * inverse
            if n == 4:
                w = jnp.where(last_z, 0.0, w)
            if n == 5:
                w = jnp.where(first_z, 0.0, w)
            coef[n, x] = w
        coef[6, x] = 2.0 * inverse
        recip = 1.0 / jnp.where(inside, e, 1.0)
        rate[x] = (DT * VISC) * total * recip
        pull[x] = (DT * DRAG) * recip
        return carry

    lax.fori_loop(WX - 1, WX + bx + 1, weights, 0, unroll=5)

    def stencil(field, x):
        v = field[x]
        return v, (((coef[0, x] * field[x + 1] + coef[1, x] * field[x - 1])
                    + (coef[2, x] * up_y(v) + coef[3, x] * down_y(v)))
                   + (coef[4, x] * up_z(v) + coef[5, x] * down_z(v)))

    for step in range(STEPS):
        v = (v1, v2)[step]
        pin = (pin1, pin2)[step]
        src = (src1, src2)[step]

        def predict(x, carry):
            s, r, g, e = solid[x], rate[x], pull[x], eps[x]
            for d in range(3):
                old, mean = stencil(v.at[d], x)
                new = old + r * (mean - old) + g * (mf[d, x] - s * old)
                guess[d, x] = new
                flux[d, x] = e * new
            return carry

        lax.fori_loop(WX - 1, WX + bx + 1, predict, 0, unroll=5)

        def balance(x, carry):
            f1, f2 = flux[1, x], flux[2, x]
            out = ((flux[0, x + 1] - flux[0, x - 1]) + (up_y(f1) - down_y(f1))
                   + (jnp.where(last_z, 0.0, up_z(f2)) - jnp.where(first_z, 0.0, down_z(f2))))
            src[x, own_y, :] = (0.5 / DT) * out[WY:WY + by]
            return carry

        lax.fori_loop(WX, WX + bx, balance, 0, unroll=8)
        start(h_src[step])
        if step == 0:
            arrive(h_rest)
            for low in (0, WX + bx + 2):
                lax.fori_loop(low, low + WX - 2, voidage, 0, unroll=3)
            for low in (1, WX + bx + 1):
                lax.fori_loop(low, low + WX - 2, weights, 0, unroll=3)
        arrive(h_p[step])
        arrive(h_src[step])

        def scale(x, carry):
            sp[x] = src[x] * coef[6, x]
            return carry

        lax.fori_loop(1, ex - 1, scale, 0, unroll=8)

        held = pin
        for sweep in range(SWEEPS):
            into = (pa, pb)[sweep % 2]

            def relax(x, carry):
                _, mean = stencil(held, x)
                into[x] = mean - sp[x]
                return carry

            lax.fori_loop(1 + sweep, ex - 1 - sweep, relax, 0, unroll=4)
            held = into

        final = step == STEPS - 1

        def correct(x, carry):
            p = held[x]
            slopes = [held[x + 1] - held[x - 1], up_y(p) - down_y(p),
                      jnp.where(last_z, 0.0, up_z(p)) - jnp.where(first_z, 0.0, down_z(p))]
            for d in range(3):
                new = (guess[d, x] - (0.5 * DT) * slopes[d])[WY:WY + by]
                if final:
                    vel_out[d, x - WX] = new
                else:
                    v2[d, x, own_y, :] = new
            if final:
                p_out[x - WX] = p[WY:WY + by]
            else:
                pin2[x, own_y, :] = p[WY:WY + by]
            return carry

        lax.fori_loop(WX, WX + bx, correct, 0, unroll=4)
        if not final:
            start(h_vel[step + 1])
            start(h_p[step + 1])
            arrive(h_vel[step + 1])

    for f in range(4):
        grid = (vel_out[f] if f < 3 else eps[own_x, own_y, :]).reshape(columns, nz)
        high, low = split(grid.T)
        ft[pl.ds(f * nz, nz), :] = jnp.concatenate([high.astype(BF16), low.astype(BF16)], axis=1)

    def gather(b, carry):
        hot = jnp.where(rk[b, 0:1, :] == column_of, 1.0, 0.0).astype(BF16)
        hot_z = rk[b, 1:2, :] == depth_of
        wide = jnp.dot(ft[...], jnp.concatenate([hot, hot], axis=0), preferred_element_type=F32)
        at = [jnp.sum(jnp.where(hot_z, wide[f * nz:(f + 1) * nz], 0.0), axis=0, keepdims=True) for f in range(4)]
        scaled = rk[b, 2:3, :] * DRAG
        for d in range(3):
            dk[b, d:d + 1, :] = scaled * (at[d] - rk[b, 3 + d:4 + d, :]) / at[3]
        return carry

    def giving(k):
        return particles(k, dk.at[lax.rem(iy + k, n_gy)], rd.at[iy], 1)

    def getting(k):
        return particles(k, dk.at[0], rd.at[lax.rem(iy + n_gy - k, n_gy)], 1)

    def gather_for(k, carry):
        gather(lax.rem(iy + k, n_gy), carry)
        giving(k).start()
        return carry

    lax.fori_loop(1, n_gy, gather_for, 0)
    gather(iy, 0)
    rd[iy] = dk[iy]
    for h in sent:
        for axis in "xyc":
            h.each(axis, lambda c, _: c.wait_send())
    for k in range(1, n_gy):
        outgoing(k).wait_send()
        getting(k).wait_recv()
        giving(k).wait_send()
    for c in range(n_gy):
        for d in range(3):
            drag_out[d, pl.ds(c, 1), :] = rd[c, d:d + 1, :]


def solution(mesh):
    n_gx, n_gy = mesh.shape["gx"], mesh.shape["gy"]

    def per_device(velocity, pressure, part_cell, part_count, grain_velocities, part_vol):
        bx, by, nz = pressure.shape
        slots = part_vol.shape[-1]
        ext = (bx + 2 * WX, by + 2 * WY, nz)
        vmem = pl.BlockSpec(memory_space=pltpu.VMEM)

        def field(*lead):
            return pltpu.VMEM(lead + ext, F32)

        def kernel(*refs):
            body(n_gx, n_gy, *refs)

        v, p, drag = pl.pallas_call(
            kernel,
            name="interval",
            out_shape=(
                jax.ShapeDtypeStruct(velocity.shape, F32),
                jax.ShapeDtypeStruct(pressure.shape, F32),
                jax.ShapeDtypeStruct((3, n_gy, slots), F32),
            ),
            in_specs=[pl.BlockSpec(memory_space=pltpu.SMEM)] + [vmem] * 5,
            out_specs=(vmem,) * 3,
            scratch_shapes=[
                field(3), field(3), field(), field(), field(), field(), field(), field(), field(),
                field(), field(3), field(), field(7), field(), field(), field(3), field(3),
                pltpu.VMEM((4 * bx * by, nz), F32),
                pltpu.VMEM((n_gy, ROWS, slots), F32),
                pltpu.VMEM((n_gy, ROWS, slots), F32),
                pltpu.VMEM((n_gy, 3, slots), F32),
                pltpu.VMEM((n_gy, 3, slots), F32),
                pltpu.VMEM((4 * nz, 2 * bx * by), BF16),
                pltpu.VMEM((14, 4, 16, nz), F32),
                pltpu.VMEM((14, 4, 16, nz), F32),
                pltpu.SemaphoreType.DMA((14, 8)),
                pltpu.SemaphoreType.DMA((14, 8)),
                pltpu.SemaphoreType.DMA((2, n_gy)),
                pltpu.SemaphoreType.DMA((2, n_gy)),
            ],
            compiler_params=pltpu.CompilerParams(
                collective_id=0, has_side_effects=True, vmem_limit_bytes=56 * 1024 * 1024
            ),
        )(
            part_count.reshape(n_gy),
            velocity,
            pressure,
            part_cell.reshape(n_gy, slots),
            grain_velocities.reshape(n_gy, 3, slots).transpose(1, 0, 2),
            part_vol.reshape(n_gy, slots),
        )
        return v, p, drag.transpose(1, 0, 2).reshape(grain_velocities.shape)

    placed = (
        P(None, "gx", "gy", None),
        P("gx", "gy", None),
        P("gx", "gy", None, None),
        P("gx", "gy", None),
        P("gx", "gy", None, None, None),
        P("gx", "gy", None, None),
    )
    return jax.shard_map(
        per_device,
        mesh=mesh,
        in_specs=placed,
        out_specs=(P(None, "gx", "gy", None), P("gx", "gy", None), P("gx", "gy", None, None, None)),
        check_vma=False,
    )
```

profile of v0, /device:TPU:0, one launch (start us, length us, event | category | flops | bytes accessed | tf_op | source)
XLA Modules:
  0.0 57.9 jit_solution(6846987903027714592)
XLA Ops:
  0.6 54.0 %interval.1 = (f32[3,8,16,256]{3,2,1,0:T(8,128)}, f32[8,16,256]{2,1,0:T(8,128)}, f32[3,8,512]{2,1,0:T(8,128)}) custom-call(s32[8]{0:T(128)} %bitcast.13, f32[3,8,16,256]{3,2,1,0:T(8,128)} %refs_1_.1, f32[8,16,256]{2,1,0:T(8,128)} %refs_2_.1, s32[8,512]{1,0:T(8,128)} %bitcast.11, f32[3,8,512]{2,1,0:T(8,128)} %bitcast.10, f32[8,512]{1,0:T(8,128)} %bitcast.12), custom_call_target="tpu_custom_call" | custom-call | tf_op jit(solution)/shard_map/interval/pallas_call | solution.py:413
  54.7 0.0 copy-start
  54.7 1.8 %copy.12 = f32[3,8,16,256]{3,2,1,0:T(8,128)} copy(f32[3,8,16,256]{3,2,1,0:T(8,128)} %get-tuple-element.12) | data formatting | bytes 786432
  56.5 0.0 copy-done
  56.5 0.0 copy-start.1
  56.5 0.7 %copy.13 = f32[8,16,256]{2,1,0:T(8,128)} copy(f32[8,16,256]{2,1,0:T(8,128)S(1)} %copy-done) | data formatting | bytes 262144
  57.1 0.1 copy-done.1
  57.3 0.6 %copy.14 = f32[1,1,8,3,512]{4,2,3,1,0:T(8,128)} copy(f32[1,1,8,3,512]{4,2,3,1,0:T(8,128)S(1)} %bitcast.9) | data formatting | bytes 98304
Async XLA Ops:
  54.7 1.8 %copy-start = (f32[8,16,256]{2,1,0:T(8,128)S(1)}, f32[8,16,256]{2,1,0:T(8,128)}, u32[]{:S(2)}) copy-start(f32[8,16,256]{2,1,0:T(8,128)} %get-tuple-element.13) | copy-start | bytes 393220
  56.5 0.8 %copy-start.1 = (f32[3,8,512]{2,1,0:T(8,128)S(1)}, f32[3,8,512]{2,1,0:T(8,128)}, u32[]{:S(2)}) copy-start(f32[3,8,512]{2,1,0:T(8,128)} %get-tuple-element.8) | copy-start | bytes 147460
where the time goes:
time: 58.1 us; the launch traced here: 57.9 us
  Pallas kernels  54 us (93%)
  local copies, waits for them, and re-layouts  3.22 us (6%)
  between operations  0.65 us (1%)
    pallas_call x1, Pallas kernels, per_device(): pl.pallas_call(kernel, name='interval', out_shape=(jax.ShapeDtypeStruct(v...  54 us
    unnamed x7, local copies, waits for them, and re-layouts  3.22 us

commit v1 on v0

--- a/solution.py
+++ b/solution.py
@@ -14,7 +14,7 @@
 
 WX = SWEEPS + 1
 WY = 8
-ROWS = 8
+ROWS = 5
 
 MESH = pl.DeviceIdType.MESH
 CORNERS = ((0, 0), (0, 1), (1, 0), (1, 1))
@@ -27,25 +27,41 @@
     return high, value - high
 
 
-def body(n_gx, n_gy, count_ref, vel_ref, p_ref, cell_ref, gv_ref, vol_ref,
-         vel_out, p_out, drag_out,
+def mate(i, k, n):
+    if n & (n - 1):
+        return lax.rem(i + k, n)
+    bit, flip = 1, 0
+    while bit < n:
+        flip = flip + bit * ((i // bit + k // bit) % 2)
+        bit *= 2
+    return flip
+
+
+def body(n_gx, n_gy, count_ref, vel_hbm, p_hbm, cell_hbm, gv_hbm, vol_hbm,
+         vel_out, p_out, drag_out, cell_ref, gv_ref, vol_ref, fetch_sem,
          v1, v2, pin1, pin2, pa, pb, src1, src2, sp, solid, mf, eps, coef, rate, pull,
          guess, flux, dep, pk, rk, dk, rd, ft, corner_out, corner_in, field_send, field_recv, part_send, part_recv):
-    bx, by, nz = p_ref.shape
+    bx, by, nz = p_hbm.shape
     ex, ey = bx + 2 * WX, by + 2 * WY
-    slots = vol_ref.shape[-1]
+    slots = vol_hbm.shape[-1]
     columns = bx * by
     ix, iy = lax.axis_index("gx"), lax.axis_index("gy")
     has = {("x", 0): ix > 0, ("x", 1): ix < n_gx - 1, ("y", 0): iy > 0, ("y", 1): iy < n_gy - 1}
     peer = {("x", 0): (ix - 1, iy), ("x", 1): (ix + 1, iy), ("y", 0): (ix, iy - 1), ("y", 1): (ix, iy + 1)}
     own_x, own_y = pl.ds(WX, bx), pl.ds(WY, by)
 
+    def to_mate(k):
+        return mate(iy, k, n_gy)
+
+    def from_mate(k):
+        return to_mate(k) if n_gy & (n_gy - 1) == 0 else lax.rem(iy + n_gy - k, n_gy)
+
     def beyond(corner):
         return ix + (2 * corner[0] - 1), iy + (2 * corner[1] - 1)
 
     barrier = pltpu.get_barrier_semaphore()
     for k in range(1, n_gy):
-        pl.semaphore_signal(barrier, inc=1, device_id=(ix, lax.rem(iy + k, n_gy)), device_id_type=MESH)
+        pl.semaphore_signal(barrier, inc=1, device_id=(ix, to_mate(k)), device_id_type=MESH)
     for side in (0, 1):
         @pl.when(has["x", side])
         def _():
@@ -55,16 +71,11 @@
         def _():
             pl.semaphore_signal(barrier, inc=1, device_id=beyond(corner), device_id_type=MESH)
 
-    slot = lax.broadcasted_iota(jnp.int32, (1, slots), 1)
-    for c in range(n_gy):
-        cell = cell_ref[pl.ds(c, 1), :]
-        column = lax.div(cell, nz)
-        pk[c, 0:1, :] = column.astype(F32)
-        pk[c, 1:2, :] = (cell - column * nz).astype(F32)
-        pk[c, 2:3, :] = jnp.where(slot < count_ref[c], vol_ref[pl.ds(c, 1), :], 0.0)
-        for d in range(3):
-            pk[c, 3 + d:4 + d, :] = gv_ref[d, pl.ds(c, 1), :]
-        pk[c, 6:8, :] = jnp.zeros((2, slots), F32)
+    fetches = [(cell_hbm, cell_ref), (vol_hbm, vol_ref), (gv_hbm, gv_ref)]
+    fetches += [(vel_hbm.at[d], v1.at[d, own_x, own_y]) for d in range(3)] + [(p_hbm, pin1.at[own_x, own_y])]
+    fetches = [pltpu.make_async_copy(source, landing, fetch_sem.at[n]) for n, (source, landing) in enumerate(fetches)]
+    for fetch in fetches:
+        fetch.start()
 
     fields = [v1.at[d] for d in range(3)] + [v2.at[d] for d in range(3)] + [mf.at[d] for d in range(3)]
     fields += [pin1, pin2, src1, src2, solid]
@@ -81,6 +92,15 @@
                 at = 0 if side == 0 else WY + by
                 field[:, pl.ds(at, WY), :] = jnp.zeros((ex, WY, nz), F32)
 
+    for fetch in fetches[:3]:
+        fetch.wait()
+    slot = lax.broadcasted_iota(jnp.int32, (1, slots), 1)
+    for c in range(n_gy):
+        pk[c, 0:1, :] = cell_ref[pl.ds(c, 1), :].astype(F32)
+        pk[c, 1:2, :] = jnp.where(slot < count_ref[c], vol_ref[pl.ds(c, 1), :], 0.0)
+        for d in range(3):
+            pk[c, 2 + d:3 + d, :] = gv_ref[d, pl.ds(c, 1), :]
+
     x_peers = jnp.where(ix > 0, 1, 0) + jnp.where(ix < n_gx - 1, 1, 0)
     y_peers = jnp.where(iy > 0, 1, 0) + jnp.where(iy < n_gy - 1, 1, 0)
     pl.semaphore_wait(barrier, n_gy - 1 + x_peers * (1 + y_peers))
@@ -88,21 +108,21 @@
     def particles(k, source, landing, bank):
         return pltpu.make_async_remote_copy(
             src_ref=source, dst_ref=landing, send_sem=part_send.at[bank, k], recv_sem=part_recv.at[bank, k],
-            device_id=(ix, lax.rem(iy + k, n_gy)), device_id_type=MESH)
+            device_id=(ix, to_mate(k)), device_id_type=MESH)
 
     def outgoing(k):
-        return particles(k, pk.at[lax.rem(iy + k, n_gy)], rk.at[iy], 0)
+        return particles(k, pk.at[to_mate(k)], rk.at[iy], 0)
 
     def incoming(k):
-        return particles(k, pk.at[0], rk.at[lax.rem(iy + n_gy - k, n_gy)], 0)
-
-    for k in range(1, n_gy):
+        return particles(k, pk.at[0], rk.at[from_mate(k)], 0)
+
+    for k in range(n_gy - 1, 0, -1):
         outgoing(k).start()
     rk[iy] = pk[iy]
 
     class Halo:
-        def __init__(self, slot, ref, width, reach=0, own=None, axes="xy", skip=0):
-            self.slot, self.ref, self.width, self.own, self.axes, self.skip = slot, ref, width, own, axes, skip
+        def __init__(self, slot, ref, width, rows=0, reach=0, axes="xy", skip=0):
+            self.slot, self.ref, self.width, self.span, self.axes, self.skip = slot, ref, width, rows, axes, skip
             self.rows = [(i, j) for i in range(reach) for j in range(reach) if i + j + 2 <= reach]
 
         def copy(self, index, source, landing, to):
@@ -113,20 +133,14 @@
         def x_copy(self, side):
             w, skip = self.width, self.skip
             at = skip if side == 0 else bx - w - skip
-            if self.own is None:
-                source = self.ref.at[pl.ds(WX + at, w), own_y]
-            else:
-                source = self.own.at[pl.ds(at, w)]
+            source = self.ref.at[pl.ds(WX + at, w), own_y]
             landing = self.ref.at[pl.ds(WX + bx + skip if side == 0 else WX - w - skip, w), own_y]
             return self.copy(side, source, landing, peer["x", side])
 
         def y_copy(self, side):
-            at = 0 if side == 0 else by - WY
-            if self.own is None:
-                source = self.ref.at[own_x, pl.ds(WY + at, WY)]
-            else:
-                source = self.own.at[:, pl.ds(at, WY)]
-            landing = self.ref.at[own_x, pl.ds(WY + by if side == 0 else 0, WY)]
+            h = self.span
+            source = self.ref.at[own_x, pl.ds(WY if side == 0 else WY + by - h, h)]
+            landing = self.ref.at[own_x, pl.ds(WY + by if side == 0 else WY - h, h)]
             return self.copy(2 + side, source, landing, peer["y", side])
 
         def c_copy(self, corner):
@@ -180,27 +194,33 @@
         for h in halos:
             h.each("c", h.unpack, flip=True)
 
-    h_vel = [[Halo(0, v1.at[0], 2, 2, vel_ref.at[0]), Halo(1, v1.at[1], 1, 2, vel_ref.at[1]), Halo(2, v1.at[2], 1, 0, vel_ref.at[2])],
-             [Halo(3, v2.at[0], 2, 2), Halo(4, v2.at[1], 1, 2), Halo(5, v2.at[2], 1)]]
-    h_p = [[Halo(6, pin1, WX, WX, p_ref)], [Halo(7, pin2, WX, WX)]]
-    h_src = [[Halo(8, src1, SWEEPS, SWEEPS)], [Halo(9, src2, SWEEPS, SWEEPS)]]
-    h_solid = [Halo(10, solid, 2, WX)]
+    h_vel = [[Halo(0, v1.at[0], 2, 1, 2), Halo(1, v1.at[1], 1, 2, 2), Halo(2, v1.at[2], 1, 1)],
+             [Halo(3, v2.at[0], 2, 1, 2), Halo(4, v2.at[1], 1, 2, 2), Halo(5, v2.at[2], 1, 1)]]
+    h_p = [[Halo(6, pin1, WX, WX, WX)], [Halo(7, pin2, WX, WX, WX)]]
+    h_src = [[Halo(8, src1, SWEEPS, SWEEPS, SWEEPS)], [Halo(9, src2, SWEEPS, SWEEPS, SWEEPS)]]
+    h_solid = [Halo(10, solid, 2, WX, WX)]
     h_rest = [Halo(13, solid, WX - 2, axes="x", skip=2)]
-    h_mf = [Halo(11, mf.at[0], 1, axes="x"), Halo(12, mf.at[1], 1, axes="y")]
-
-    for d in range(3):
-        v1[d, own_x, own_y, :] = vel_ref[d]
-    pin1[own_x, own_y, :] = p_ref[...]
+    h_mf = [Halo(11, mf.at[0], 1, axes="x"), Halo(12, mf.at[1], rows=1, width=0, axes="y")]
+
+    for fetch in fetches[3:]:
+        fetch.wait()
     start(h_vel[0] + h_p[0])
 
     column_of = lax.broadcasted_iota(jnp.int32, (columns, slots), 0).astype(F32)
     depth_of = lax.broadcasted_iota(jnp.int32, (nz, slots), 0).astype(F32)
     dep[...] = jnp.zeros_like(dep)
+
+    def where_of(b):
+        cell = rk[b, 0:1, :]
+        column = jnp.floor((cell + 0.5) * (1.0 / nz))
+        return column, cell - column * nz
+
     def deposit(b, carry):
-        hot_c = rk[b, 0:1, :] == column_of
-        hot_z = jnp.where(rk[b, 1:2, :] == depth_of, 1.0, 0.0).astype(BF16)
-        volume = rk[b, 2:3, :]
-        values = [volume] + [volume * rk[b, 3 + d:4 + d, :] for d in range(3)]
+        column, level = where_of(b)
+        hot_c = column == column_of
+        hot_z = jnp.where(level == depth_of, 1.0, 0.0).astype(BF16)
+        volume = rk[b, 1:2, :]
+        values = [volume] + [volume * rk[b, 2 + d:3 + d, :] for d in range(3)]
         parts = [split(value) for value in values]
         both = None
         for side in (0, 1):
@@ -214,7 +234,7 @@
 
     def deposit_from(k, carry):
         incoming(k).wait_recv()
-        return deposit(lax.rem(iy + n_gy - k, n_gy), carry)
+        return deposit(from_mate(k), carry)
 
     lax.fori_loop(1, n_gy, deposit_from, 0)
     solid[own_x, own_y, :] = dep[pl.ds(0, columns), :].reshape(bx, by, nz)
@@ -360,24 +380,25 @@
         ft[pl.ds(f * nz, nz), :] = jnp.concatenate([high.astype(BF16), low.astype(BF16)], axis=1)
 
     def gather(b, carry):
-        hot = jnp.where(rk[b, 0:1, :] == column_of, 1.0, 0.0).astype(BF16)
-        hot_z = rk[b, 1:2, :] == depth_of
+        column, level = where_of(b)
+        hot = jnp.where(column == column_of, 1.0, 0.0).astype(BF16)
+        hot_z = level == depth_of
         wide = jnp.dot(ft[...], jnp.concatenate([hot, hot], axis=0), preferred_element_type=F32)
         at = [jnp.sum(jnp.where(hot_z, wide[f * nz:(f + 1) * nz], 0.0), axis=0, keepdims=True) for f in range(4)]
-        scaled = rk[b, 2:3, :] * DRAG
+        scaled = rk[b, 1:2, :] * DRAG
         for d in range(3):
-            dk[b, d:d + 1, :] = scaled * (at[d] - rk[b, 3 + d:4 + d, :]) / at[3]
+            dk[b, d:d + 1, :] = scaled * (at[d] - rk[b, 2 + d:3 + d, :]) / at[3]
         return carry
 
     def giving(k):
-        return particles(k, dk.at[lax.rem(iy + k, n_gy)], rd.at[iy], 1)
+        return particles(k, dk.at[to_mate(k)], rd.at[iy], 1)
 
     def getting(k):
-        return particles(k, dk.at[0], rd.at[lax.rem(iy + n_gy - k, n_gy)], 1)
+        return particles(k, dk.at[0], rd.at[from_mate(k)], 1)
 
     def gather_for(k, carry):
-        gather(lax.rem(iy + k, n_gy), carry)
-        giving(k).start()
+        gather(to_mate(n_gy - k), carry)
+        giving(n_gy - k).start()
         return carry
 
     lax.fori_loop(1, n_gy, gather_for, 0)
@@ -395,6 +416,15 @@
             drag_out[d, pl.ds(c, 1), :] = rd[c, d:d + 1, :]
 
 
+def deliver(*refs):
+    pairs = len(refs) // 2
+    copies = [pltpu.make_async_copy(refs[n], refs[pairs + n], refs[-1].at[n]) for n in range(pairs)]
+    for copy in copies:
+        copy.start()
+    for copy in copies:
+        copy.wait()
+
+
 def solution(mesh):
     n_gx, n_gy = mesh.shape["gx"], mesh.shape["gy"]
 
@@ -403,6 +433,7 @@
         slots = part_vol.shape[-1]
         ext = (bx + 2 * WX, by + 2 * WY, nz)
         vmem = pl.BlockSpec(memory_space=pltpu.VMEM)
+        anywhere = pl.BlockSpec(memory_space=pl.ANY)
 
         def field(*lead):
             return pltpu.VMEM(lead + ext, F32)
@@ -414,13 +445,17 @@
             kernel,
             name="interval",
             out_shape=(
-                jax.ShapeDtypeStruct(velocity.shape, F32),
-                jax.ShapeDtypeStruct(pressure.shape, F32),
-                jax.ShapeDtypeStruct((3, n_gy, slots), F32),
+                pltpu.VMEM(velocity.shape, F32),
+                pltpu.VMEM(pressure.shape, F32),
+                pltpu.VMEM((3, n_gy, slots), F32),
             ),
-            in_specs=[pl.BlockSpec(memory_space=pltpu.SMEM)] + [vmem] * 5,
+            in_specs=[pl.BlockSpec(memory_space=pltpu.SMEM)] + [anywhere] * 5,
             out_specs=(vmem,) * 3,
             scratch_shapes=[
+                pltpu.VMEM((n_gy, slots), jnp.int32),
+                pltpu.VMEM((3, n_gy, slots), F32),
+                pltpu.VMEM((n_gy, slots), F32),
+                pltpu.SemaphoreType.DMA((7,)),
                 field(3), field(3), field(), field(), field(), field(), field(), field(), field(),
                 field(), field(3), field(), field(7), field(), field(), field(3), field(3),
                 pltpu.VMEM((4 * bx * by, nz), F32),
@@ -447,6 +482,15 @@
             grain_velocities.reshape(n_gy, 3, slots).transpose(1, 0, 2),
             part_vol.reshape(n_gy, slots),
         )
+        v, p, drag = [pltpu.with_memory_space_constraint(a, pltpu.VMEM) for a in (v, p, drag)]
+        v, p, drag = pl.pallas_call(
+            deliver,
+            name="deliver",
+            out_shape=tuple(jax.ShapeDtypeStruct(a.shape, F32) for a in (v, p, drag)),
+            in_specs=(vmem,) * 3,
+            out_specs=(anywhere,) * 3,
+            scratch_shapes=[pltpu.SemaphoreType.DMA((3,))],
+        )(v, p, drag)
         return v, p, drag.transpose(1, 0, 2).reshape(grain_velocities.shape)
 
     placed = (

time: 58.1 us -> 54.6 us (0.940)
  local copies, waits for them, and re-layouts: 3.22 us -> 0 us
    unnamed x7 -> x0, local copies, waits for them, and re-layouts: 3.22 us -> none
    pallas_call x1 -> x2, Pallas kernels: 54 us -> 53.7 us  [the longest x1 52.9 us: per_device(): pl.pallas_call(kernel, name='interval', out_shape=(pltpu.VMEM(velocity.sh...]
where the time goes in v1:
time: 54.6 us; the launch traced here: 54.3 us
  Pallas kernels  53.7 us (98%)
  between operations  0.64 us (1%)
    pallas_call x1, Pallas kernels, per_device(): pl.pallas_call(kernel, name='interval', out_shape=(pltpu.VMEM(velocity.sh...  52.9 us

profile of v1, /device:TPU:0, one launch (start us, length us, event | category | flops | bytes accessed | tf_op | source)
XLA Modules:
  0.0 54.3 jit_solution(11253104438765295487)
XLA Ops:
  0.6 52.9 %interval.1 = (f32[3,8,16,256]{3,2,1,0:T(8,128)S(1)}, f32[8,16,256]{2,1,0:T(8,128)S(1)}, f32[3,8,512]{2,1,0:T(8,128)S(1)}) custom-call(s32[8]{0:T(128)} %bitcast.12, f32[3,8,16,256]{3,2,1,0:T(8,128)} %refs_1_.1, f32[8,16,256]{2,1,0:T(8,128)} %refs_2_.1, s32[8,512]{1,0:T(8,128)} %bitcast.10, f32[3,8,512]{2,1,0:T(8,128)} %bitcast.9, f32[8,512]{1,0:T(8,128)} %bitcast.11), custom_call_target="tpu_custom_call" | custom-call | tf_op jit(solution)/shard_map/interval/pallas_call | solution.py:444
  53.5 0.8 %deliver.1 = (f32[3,8,16,256]{3,2,1,0:T(8,128)}, f32[8,16,256]{2,1,0:T(8,128)}, f32[3,8,512]{2,1,0:T(8,128)}) custom-call(f32[3,8,16,256]{3,2,1,0:T(8,128)S(1)} %get-tuple-element.9.refs_0_, f32[8,16,256]{2,1,0:T(8,128)S(1)} %get-tuple-element.10.refs_1_, f32[3,8,512]{2,1,0:T(8,128)S(1)} %get-tuple-element.11.refs_2_), custom_call_target="tpu_custom_call" | custom-call | tf_op jit(solution)/shard_map/deliver/pallas_call | solution.py:486

commit v2 on v1

--- a/solution.py
+++ b/solution.py
@@ -40,7 +40,7 @@
 def body(n_gx, n_gy, count_ref, vel_hbm, p_hbm, cell_hbm, gv_hbm, vol_hbm,
          vel_out, p_out, drag_out, cell_ref, gv_ref, vol_ref, fetch_sem,
          v1, v2, pin1, pin2, pa, pb, src1, src2, sp, solid, mf, eps, coef, rate, pull,
-         guess, flux, dep, pk, rk, dk, rd, ft, corner_out, corner_in, field_send, field_recv, part_send, part_recv):
+         guess, flux, dep, pk, rk, dk, rd, ft, pull_of, corner_out, corner_in, field_send, field_recv, part_send, part_recv):
     bx, by, nz = p_hbm.shape
     ex, ey = bx + 2 * WX, by + 2 * WY
     slots = vol_hbm.shape[-1]
@@ -138,14 +138,14 @@
             return self.copy(side, source, landing, peer["x", side])
 
         def y_copy(self, side):
-            h = self.span
-            source = self.ref.at[own_x, pl.ds(WY if side == 0 else WY + by - h, h)]
-            landing = self.ref.at[own_x, pl.ds(WY + by if side == 0 else WY - h, h)]
+            h, skip = self.span, self.skip
+            source = self.ref.at[own_x, pl.ds(WY + skip if side == 0 else WY + by - h - skip, h)]
+            landing = self.ref.at[own_x, pl.ds(WY + by + skip if side == 0 else WY - h - skip, h)]
             return self.copy(2 + side, source, landing, peer["y", side])
 
         def c_copy(self, corner):
             n = 2 * corner[0] + corner[1]
-            size = -(-len(self.rows) // 8) * 8
+            size = len(self.rows)
             return self.copy(4 + n, corner_out.at[self.slot, n, pl.ds(0, size)],
                              corner_in.at[self.slot, n, pl.ds(0, size)], beyond(corner))
 
@@ -154,7 +154,7 @@
                 for n, (i, j) in enumerate(self.rows):
                     x = WX + (i if corner[0] == 0 else bx - 1 - i)
                     y = WY + (j if corner[1] == 0 else by - 1 - j)
-                    corner_out[self.slot, 2 * corner[0] + corner[1], n:n + 1, :] = self.ref[x, y:y + 1, :]
+                    corner_out[self.slot, 2 * corner[0] + corner[1], n] = self.ref[x, y:y + 1, :]
 
         def each(self, axis, act, flip=False):
             if axis == "c":
@@ -175,7 +175,7 @@
             for n, (i, j) in enumerate(self.rows):
                 x = WX + bx + i if corner[0] == 0 else WX - 1 - i
                 y = WY + by + j if corner[1] == 0 else WY - 1 - j
-                self.ref[x, y:y + 1, :] = corner_in[self.slot, 2 * corner[0] + corner[1], n:n + 1, :]
+                self.ref[x, y:y + 1, :] = corner_in[self.slot, 2 * corner[0] + corner[1], n]
 
     sent = []
 
@@ -196,7 +196,7 @@
 
     h_vel = [[Halo(0, v1.at[0], 2, 1, 2), Halo(1, v1.at[1], 1, 2, 2), Halo(2, v1.at[2], 1, 1)],
              [Halo(3, v2.at[0], 2, 1, 2), Halo(4, v2.at[1], 1, 2, 2), Halo(5, v2.at[2], 1, 1)]]
-    h_p = [[Halo(6, pin1, WX, WX, WX)], [Halo(7, pin2, WX, WX, WX)]]
+    h_p = [[Halo(6, pin1, WX, WX, WX)], [Halo(7, pin2, WX - 1, WX - 1, WX, skip=1)]]
     h_src = [[Halo(8, src1, SWEEPS, SWEEPS, SWEEPS)], [Halo(9, src2, SWEEPS, SWEEPS, SWEEPS)]]
     h_solid = [Halo(10, solid, 2, WX, WX)]
     h_rest = [Halo(13, solid, WX - 2, axes="x", skip=2)]
@@ -298,6 +298,23 @@
                     + (coef[2, x] * up_y(v) + coef[3, x] * down_y(v)))
                    + (coef[4, x] * up_z(v) + coef[5, x] * down_z(v)))
 
+    def wide(b, tables):
+        column, level = where_of(b)
+        hot = jnp.where(column == column_of, 1.0, 0.0).astype(BF16)
+        found = jnp.dot(tables, jnp.concatenate([hot, hot], axis=0), preferred_element_type=F32)
+        hot_z = level == depth_of
+        return [jnp.sum(jnp.where(hot_z, found[n:n + nz], 0.0), axis=0, keepdims=True)
+                for n in range(0, found.shape[0], nz)]
+
+    def table(grid):
+        high, low = split(grid.reshape(columns, nz).T)
+        return jnp.concatenate([high.astype(BF16), low.astype(BF16)], axis=1)
+
+    def porosity(b, carry):
+        at, = wide(b, ft[pl.ds(3 * nz, nz), :])
+        pull_of[b] = rk[b, 1:2, :] * DRAG / at
+        return carry
+
     for step in range(STEPS):
         v = (v1, v2)[step]
         pin = (pin1, pin2)[step]
@@ -329,6 +346,9 @@
                 lax.fori_loop(low, low + WX - 2, voidage, 0, unroll=3)
             for low in (1, WX + bx + 1):
                 lax.fori_loop(low, low + WX - 2, weights, 0, unroll=3)
+        else:
+            ft[pl.ds(3 * nz, nz), :] = table(eps[own_x, own_y, :])
+            lax.fori_loop(0, n_gy, porosity, 0)
         arrive(h_p[step])
         arrive(h_src[step])
 
@@ -365,29 +385,25 @@
             if final:
                 p_out[x - WX] = p[WY:WY + by]
             else:
-                pin2[x, own_y, :] = p[WY:WY + by]
+                for low, high in ((WY - 1, WY), (WY, WY + by), (WY + by, WY + by + 1)):
+                    pin2[x, low:high, :] = p[low:high]
             return carry
 
         lax.fori_loop(WX, WX + bx, correct, 0, unroll=4)
         if not final:
+            for x in (WX - 1, WX + bx):
+                pin2[x, own_y, :] = held[x, own_y, :]
             start(h_vel[step + 1])
             start(h_p[step + 1])
             arrive(h_vel[step + 1])
 
-    for f in range(4):
-        grid = (vel_out[f] if f < 3 else eps[own_x, own_y, :]).reshape(columns, nz)
-        high, low = split(grid.T)
-        ft[pl.ds(f * nz, nz), :] = jnp.concatenate([high.astype(BF16), low.astype(BF16)], axis=1)
+    for d in range(3):
+        ft[pl.ds(d * nz, nz), :] = table(vel_out[d])
 
     def gather(b, carry):
-        column, level = where_of(b)
-        hot = jnp.where(column == column_of, 1.0, 0.0).astype(BF16)
-        hot_z = level == depth_of
-        wide = jnp.dot(ft[...], jnp.concatenate([hot, hot], axis=0), preferred_element_type=F32)
-        at = [jnp.sum(jnp.where(hot_z, wide[f * nz:(f + 1) * nz], 0.0), axis=0, keepdims=True) for f in range(4)]
-        scaled = rk[b, 1:2, :] * DRAG
+        at = wide(b, ft[pl.ds(0, 3 * nz), :])
         for d in range(3):
-            dk[b, d:d + 1, :] = scaled * (at[d] - rk[b, 2 + d:3 + d, :]) / at[3]
+            dk[b, d:d + 1, :] = pull_of[b] * (at[d] - rk[b, 2 + d:3 + d, :])
         return carry
 
     def giving(k):
@@ -464,8 +480,9 @@
                 pltpu.VMEM((n_gy, 3, slots), F32),
                 pltpu.VMEM((n_gy, 3, slots), F32),
                 pltpu.VMEM((4 * nz, 2 * bx * by), BF16),
-                pltpu.VMEM((14, 4, 16, nz), F32),
-                pltpu.VMEM((14, 4, 16, nz), F32),
+                pltpu.VMEM((n_gy, 1, slots), F32),
+                pltpu.VMEM((14, 4, WX * (WX - 1) // 2, 1, nz), F32),
+                pltpu.VMEM((14, 4, WX * (WX - 1) // 2, 1, nz), F32),
                 pltpu.SemaphoreType.DMA((14, 8)),
                 pltpu.SemaphoreType.DMA((14, 8)),
                 pltpu.SemaphoreType.DMA((2, n_gy)),

time: 54.6 us -> 49.8 us (0.912)
  Pallas kernels: 53.7 us -> 49 us
    pallas_call x1, Pallas kernels: 52.9 us -> 48.1 us  [per_device(): pl.pallas_call(kernel, name='interval', out_shape=(pltpu.VMEM(velocity.sh...]
where the time goes in v2:
time: 49.8 us; the launch traced here: 49.6 us
  Pallas kernels  49 us (98%)
  between operations  0.64 us (1%)
    pallas_call x1, Pallas kernels, per_device(): pl.pallas_call(kernel, name='interval', out_shape=(pltpu.VMEM(velocity.sh...  48.1 us

profile of v2, /device:TPU:0, one launch (start us, length us, event | category | flops | bytes accessed | tf_op | source)
XLA Modules:
  0.0 49.6 jit_solution(10552914718154674413)
XLA Ops:
  0.6 48.1 %interval.1 = (f32[3,8,16,256]{3,2,1,0:T(8,128)S(1)}, f32[8,16,256]{2,1,0:T(8,128)S(1)}, f32[3,8,512]{2,1,0:T(8,128)S(1)}) custom-call(s32[8]{0:T(128)} %bitcast.12, f32[3,8,16,256]{3,2,1,0:T(8,128)} %refs_1_.1, f32[8,16,256]{2,1,0:T(8,128)} %refs_2_.1, s32[8,512]{1,0:T(8,128)} %bitcast.10, f32[3,8,512]{2,1,0:T(8,128)} %bitcast.9, f32[8,512]{1,0:T(8,128)} %bitcast.11), custom_call_target="tpu_custom_call" | custom-call | tf_op jit(solution)/shard_map/interval/pallas_call | solution.py:460
  48.8 0.8 %deliver.1 = (f32[3,8,16,256]{3,2,1,0:T(8,128)}, f32[8,16,256]{2,1,0:T(8,128)}, f32[3,8,512]{2,1,0:T(8,128)}) custom-call(f32[3,8,16,256]{3,2,1,0:T(8,128)S(1)} %get-tuple-element.9.refs_0_, f32[8,16,256]{2,1,0:T(8,128)S(1)} %get-tuple-element.10.refs_1_, f32[3,8,512]{2,1,0:T(8,128)S(1)} %get-tuple-element.11.refs_2_), custom_call_target="tpu_custom_call" | custom-call | tf_op jit(solution)/shard_map/deliver/pallas_call | solution.py:503

commit v3 on v2

--- a/solution.py
+++ b/solution.py
@@ -121,9 +121,9 @@
     rk[iy] = pk[iy]
 
     class Halo:
-        def __init__(self, slot, ref, width, rows=0, reach=0, axes="xy", skip=0):
+        def __init__(self, slot, ref, width, rows=0, reach=0, axes="xy", skip=0, over=0):
             self.slot, self.ref, self.width, self.span, self.axes, self.skip = slot, ref, width, rows, axes, skip
-            self.rows = [(i, j) for i in range(reach) for j in range(reach) if i + j + 2 <= reach]
+            self.rows = [(i, j) for i in range(reach) for j in range(reach) if over < i + j + 2 <= reach]
 
         def copy(self, index, source, landing, to):
             return pltpu.make_async_remote_copy(
@@ -187,19 +187,19 @@
                 h.each(axis, lambda c, _: c.start())
         sent.extend(halos)
 
-    def arrive(halos):
-        for h in halos:
-            h.each("y", lambda c, _: c.wait_recv(), flip=True)
-            h.each("x", lambda c, _: c.wait_recv(), flip=True)
-        for h in halos:
-            h.each("c", h.unpack, flip=True)
+    def arrive(halos, axes="yxc"):
+        for axis in axes:
+            for h in halos:
+                h.each(axis, h.unpack if axis == "c" else lambda c, _: c.wait_recv(), flip=True)
 
     h_vel = [[Halo(0, v1.at[0], 2, 1, 2), Halo(1, v1.at[1], 1, 2, 2), Halo(2, v1.at[2], 1, 1)],
              [Halo(3, v2.at[0], 2, 1, 2), Halo(4, v2.at[1], 1, 2, 2), Halo(5, v2.at[2], 1, 1)]]
     h_p = [[Halo(6, pin1, WX, WX, WX)], [Halo(7, pin2, WX - 1, WX - 1, WX, skip=1)]]
-    h_src = [[Halo(8, src1, SWEEPS, SWEEPS, SWEEPS)], [Halo(9, src2, SWEEPS, SWEEPS, SWEEPS)]]
-    h_solid = [Halo(10, solid, 2, WX, WX)]
-    h_rest = [Halo(13, solid, WX - 2, axes="x", skip=2)]
+    near = SWEEPS // 2
+    h_src = [[Halo(8, src1, near, SWEEPS, SWEEPS)], [Halo(9, src2, near, SWEEPS, SWEEPS)]]
+    h_far = [[Halo(14, src1, SWEEPS - near, axes="x", skip=near)], [Halo(15, src2, SWEEPS - near, axes="x", skip=near)]]
+    h_solid = [Halo(10, solid, 2, WX, 2)]
+    h_rest = [Halo(13, solid, WX - 2, reach=WX, axes="x", skip=2, over=2)]
     h_mf = [Halo(11, mf.at[0], 1, axes="x"), Halo(12, mf.at[1], rows=1, width=0, axes="y")]
 
     for fetch in fetches[3:]:
@@ -242,8 +242,6 @@
         mf[d, own_x, own_y, :] = dep[pl.ds((1 + d) * columns, columns), :].reshape(bx, by, nz)
     start(h_solid + h_mf)
     start(h_rest)
-    arrive(h_solid + h_mf)
-    arrive(h_vel[0])
 
     row = lax.broadcasted_iota(jnp.int32, (ey, nz), 0)
     depth = lax.broadcasted_iota(jnp.int32, (ey, nz), 1)
@@ -254,7 +252,12 @@
         eps[x] = jnp.maximum(1.0 - solid[x], FLOOR) * (row_in * jnp.where(x_in, 1.0, 0.0))
         return carry
 
-    lax.fori_loop(WX - 2, WX + bx + 2, voidage, 0, unroll=4)
+    def sweep_over(act, spans, unroll):
+        for first, end in spans:
+            if first < end:
+                lax.fori_loop(first, end, act, 0, unroll=min(unroll, end - first))
+
+    low, high = WX, WX + bx
 
     def up_y(v):
         return pltpu.roll(v, ey - 1, 0)
@@ -290,8 +293,6 @@
         pull[x] = (DT * DRAG) * recip
         return carry
 
-    lax.fori_loop(WX - 1, WX + bx + 1, weights, 0, unroll=5)
-
     def stencil(field, x):
         v = field[x]
         return v, (((coef[0, x] * field[x + 1] + coef[1, x] * field[x - 1])
@@ -329,8 +330,6 @@
                 flux[d, x] = e * new
             return carry
 
-        lax.fori_loop(WX - 1, WX + bx + 1, predict, 0, unroll=5)
-
         def balance(x, carry):
             f1, f2 = flux[1, x], flux[2, x]
             out = ((flux[0, x + 1] - flux[0, x - 1]) + (up_y(f1) - down_y(f1))
@@ -338,37 +337,60 @@
             src[x, own_y, :] = (0.5 / DT) * out[WY:WY + by]
             return carry
 
-        lax.fori_loop(WX, WX + bx, balance, 0, unroll=8)
+        early = h_vel[step] + (h_solid + h_mf if step == 0 else [])
+        arrive(early, "y")
+        if step == 0:
+            sweep_over(voidage, [(low, high)], 4)
+            sweep_over(weights, [(low + 1, high - 1)], 3)
+        sweep_over(predict, [(low + 1, high - 1)], 3)
+        sweep_over(balance, [(low + near, high - near)], 4)
+        start(h_far[step])
+        arrive(early, "xc")
+        if step == 0:
+            sweep_over(voidage, [(low - 2, low), (high, high + 2)], 2)
+            sweep_over(weights, [(low - 1, low + 1), (high - 1, high + 1)], 2)
+        sweep_over(predict, [(low - 1, low + 1), (high - 1, high + 1)], 2)
+        sweep_over(balance, [(low, low + near), (high - near, high)], 2)
         start(h_src[step])
+        arrive(h_src[step], "y")
         if step == 0:
             arrive(h_rest)
-            for low in (0, WX + bx + 2):
-                lax.fori_loop(low, low + WX - 2, voidage, 0, unroll=3)
-            for low in (1, WX + bx + 1):
-                lax.fori_loop(low, low + WX - 2, weights, 0, unroll=3)
+            sweep_over(voidage, [(0, low), (high, ex)], 5)
+            sweep_over(weights, [(1, low + 1), (high - 1, ex - 1)], 5)
+            arrive(h_p[step])
         else:
-            ft[pl.ds(3 * nz, nz), :] = table(eps[own_x, own_y, :])
-            lax.fori_loop(0, n_gy, porosity, 0)
-        arrive(h_p[step])
-        arrive(h_src[step])
+            arrive(h_p[step], "y")
 
         def scale(x, carry):
             sp[x] = src[x] * coef[6, x]
             return carry
 
-        lax.fori_loop(1, ex - 1, scale, 0, unroll=8)
-
-        held = pin
-        for sweep in range(SWEEPS):
-            into = (pa, pb)[sweep % 2]
+        stages = [pin] + [(pa, pb)[sweep % 2] for sweep in range(SWEEPS)]
+
+        def relaxing(sweep):
+            held, into = stages[sweep], stages[sweep + 1]
 
             def relax(x, carry):
                 _, mean = stencil(held, x)
                 into[x] = mean - sp[x]
                 return carry
 
-            lax.fori_loop(1 + sweep, ex - 1 - sweep, relax, 0, unroll=4)
-            held = into
+            return relax
+
+        inset = 0 if step == 0 else 1
+        sweep_over(scale, [(low, high)], 8)
+        for sweep in range(SWEEPS):
+            sweep_over(relaxing(sweep), [(low + sweep + inset, high - sweep - inset)], 4)
+        if step:
+            ft[pl.ds(3 * nz, nz), :] = table(eps[own_x, own_y, :])
+            lax.fori_loop(0, n_gy, porosity, 0)
+            arrive(h_p[step], "xc")
+        arrive(h_src[step], "xc")
+        arrive(h_far[step])
+        sweep_over(scale, [(1, low), (high, ex - 1)], 4)
+        for sweep in range(SWEEPS):
+            sweep_over(relaxing(sweep), [(1 + sweep, low + sweep + inset), (high - sweep - inset, ex - 1 - sweep)], 5)
+        held = stages[SWEEPS]
 
         final = step == STEPS - 1
 
@@ -395,7 +417,6 @@
                 pin2[x, own_y, :] = held[x, own_y, :]
             start(h_vel[step + 1])
             start(h_p[step + 1])
-            arrive(h_vel[step + 1])
 
     for d in range(3):
         ft[pl.ds(d * nz, nz), :] = table(vel_out[d])
@@ -481,10 +502,10 @@
                 pltpu.VMEM((n_gy, 3, slots), F32),
                 pltpu.VMEM((4 * nz, 2 * bx * by), BF16),
                 pltpu.VMEM((n_gy, 1, slots), F32),
-                pltpu.VMEM((14, 4, WX * (WX - 1) // 2, 1, nz), F32),
-                pltpu.VMEM((14, 4, WX * (WX - 1) // 2, 1, nz), F32),
-                pltpu.SemaphoreType.DMA((14, 8)),
-                pltpu.SemaphoreType.DMA((14, 8)),
+                pltpu.VMEM((16, 4, WX * (WX - 1) // 2, 1, nz), F32),
+                pltpu.VMEM((16, 4, WX * (WX - 1) // 2, 1, nz), F32),
+                pltpu.SemaphoreType.DMA((16, 8)),
+                pltpu.SemaphoreType.DMA((16, 8)),
                 pltpu.SemaphoreType.DMA((2, n_gy)),
                 pltpu.SemaphoreType.DMA((2, n_gy)),
             ],

time: 49.8 us -> 47 us (0.944)
  Pallas kernels: 49 us -> 46.1 us
    pallas_call x1, Pallas kernels: 48.1 us -> 45.3 us  [per_device(): pl.pallas_call(kernel, name='interval', out_shape=(pltpu.VMEM(velocity.sh...]
where the time goes in v3:
time: 47 us; the launch traced here: 46.7 us
  Pallas kernels  46.1 us (98%)
  between operations  0.64 us (1%)
    pallas_call x1, Pallas kernels, per_device(): pl.pallas_call(kernel, name='interval', out_shape=(pltpu.VMEM(velocity.sh...  45.3 us

profile of v3, /device:TPU:0, one launch (start us, length us, event | category | flops | bytes accessed | tf_op | source)
XLA Modules:
  0.0 46.7 jit_solution(1876172284078152597)
XLA Ops:
  0.6 45.3 %interval.1 = (f32[3,8,16,256]{3,2,1,0:T(8,128)S(1)}, f32[8,16,256]{2,1,0:T(8,128)S(1)}, f32[3,8,512]{2,1,0:T(8,128)S(1)}) custom-call(s32[8]{0:T(128)} %bitcast.12, f32[3,8,16,256]{3,2,1,0:T(8,128)} %refs_1_.1, f32[8,16,256]{2,1,0:T(8,128)} %refs_2_.1, s32[8,512]{1,0:T(8,128)} %bitcast.10, f32[3,8,512]{2,1,0:T(8,128)} %bitcast.9, f32[8,512]{1,0:T(8,128)} %bitcast.11), custom_call_target="tpu_custom_call" | custom-call | tf_op jit(solution)/shard_map/interval/pallas_call | solution.py:481
  45.9 0.8 %deliver.1 = (f32[3,8,16,256]{3,2,1,0:T(8,128)}, f32[8,16,256]{2,1,0:T(8,128)}, f32[3,8,512]{2,1,0:T(8,128)}) custom-call(f32[3,8,16,256]{3,2,1,0:T(8,128)S(1)} %get-tuple-element.9.refs_0_, f32[8,16,256]{2,1,0:T(8,128)S(1)} %get-tuple-element.10.refs_1_, f32[3,8,512]{2,1,0:T(8,128)S(1)} %get-tuple-element.11.refs_2_), custom_call_target="tpu_custom_call" | custom-call | tf_op jit(solution)/shard_map/deliver/pallas_call | solution.py:524

commit v4 on v3

--- a/solution.py
+++ b/solution.py
@@ -40,7 +40,8 @@
 def body(n_gx, n_gy, count_ref, vel_hbm, p_hbm, cell_hbm, gv_hbm, vol_hbm,
          vel_out, p_out, drag_out, cell_ref, gv_ref, vol_ref, fetch_sem,
          v1, v2, pin1, pin2, pa, pb, src1, src2, sp, solid, mf, eps, coef, rate, pull,
-         guess, flux, dep, pk, rk, dk, rd, ft, pull_of, corner_out, corner_in, field_send, field_recv, part_send, part_recv):
+         guess, flux, dep, pk, rk, dk, rd, ft, pull_of, corner_out, corner_in, passed, aside_send, aside_recv,
+         field_send, field_recv, part_send, part_recv):
     bx, by, nz = p_hbm.shape
     ex, ey = bx + 2 * WX, by + 2 * WY
     slots = vol_hbm.shape[-1]
@@ -71,6 +72,14 @@
         def _():
             pl.semaphore_signal(barrier, inc=1, device_id=beyond(corner), device_id_type=MESH)
 
+    square = n_gx == 4
+    origin, middle, target = (2, 1), (0, 3), (1, 2)
+    if square:
+        for side in (0, 1):
+            @pl.when(ix == middle[side])
+            def _():
+                pl.semaphore_signal(barrier, inc=1, device_id=(origin[side], iy), device_id_type=MESH)
+
     fetches = [(cell_hbm, cell_ref), (vol_hbm, vol_ref), (gv_hbm, gv_ref)]
     fetches += [(vel_hbm.at[d], v1.at[d, own_x, own_y]) for d in range(3)] + [(p_hbm, pin1.at[own_x, own_y])]
     fetches = [pltpu.make_async_copy(source, landing, fetch_sem.at[n]) for n, (source, landing) in enumerate(fetches)]
@@ -103,7 +112,8 @@
 
     x_peers = jnp.where(ix > 0, 1, 0) + jnp.where(ix < n_gx - 1, 1, 0)
     y_peers = jnp.where(iy > 0, 1, 0) + jnp.where(iy < n_gy - 1, 1, 0)
-    pl.semaphore_wait(barrier, n_gy - 1 + x_peers * (1 + y_peers))
+    detours = jnp.where((ix == 1) | (ix == 2), 1, 0) if square else 0
+    pl.semaphore_wait(barrier, n_gy - 1 + x_peers * (1 + y_peers) + detours)
 
     def particles(k, source, landing, bank):
         return pltpu.make_async_remote_copy(
@@ -121,8 +131,9 @@
     rk[iy] = pk[iy]
 
     class Halo:
-        def __init__(self, slot, ref, width, rows=0, reach=0, axes="xy", skip=0, over=0):
+        def __init__(self, slot, ref, width, rows=0, reach=0, axes="xy", skip=0, over=0, detour=None):
             self.slot, self.ref, self.width, self.span, self.axes, self.skip = slot, ref, width, rows, axes, skip
+            self.detour = detour if square else None
             self.rows = [(i, j) for i in range(reach) for j in range(reach) if over < i + j + 2 <= reach]
 
         def copy(self, index, source, landing, to):
@@ -136,6 +147,42 @@
             source = self.ref.at[pl.ds(WX + at, w), own_y]
             landing = self.ref.at[pl.ds(WX + bx + skip if side == 0 else WX - w - skip, w), own_y]
             return self.copy(side, source, landing, peer["x", side])
+
+        def aside(self, side):
+            held = passed.at[self.detour, pl.ds(0, self.width)]
+            at = self.skip if side == 0 else bx - self.width - self.skip
+            return pltpu.make_async_remote_copy(
+                src_ref=self.ref.at[pl.ds(WX + at, self.width), own_y], dst_ref=held,
+                send_sem=field_send.at[self.slot, side], recv_sem=aside_recv.at[self.detour],
+                device_id=(middle[side], iy), device_id_type=MESH)
+
+        def onward(self, side):
+            landing = WX + bx + self.skip if side == 0 else WX - self.width - self.skip
+            return pltpu.make_async_remote_copy(
+                src_ref=passed.at[self.detour, pl.ds(0, self.width)],
+                dst_ref=self.ref.at[pl.ds(landing, self.width), own_y],
+                send_sem=aside_send.at[self.detour], recv_sem=field_recv.at[self.slot, side],
+                device_id=(target[side], iy), device_id_type=MESH)
+
+        def send_x(self):
+            for side in (0, 1):
+                straight = has["x", side]
+                if self.detour is not None:
+                    straight = straight & (ix != origin[side])
+
+                    @pl.when(ix == origin[side])
+                    def _():
+                        self.aside(side).start()
+
+                @pl.when(straight)
+                def _():
+                    self.x_copy(side).start()
+
+        def pass_on(self, act):
+            for side in (0, 1) if self.detour is not None else ():
+                @pl.when(ix == middle[side])
+                def _():
+                    act(self, side)
 
         def y_copy(self, side):
             h, skip = self.span, self.skip
@@ -184,7 +231,10 @@
             h.pack()
         for axis in "cxy":
             for h in halos:
-                h.each(axis, lambda c, _: c.start())
+                if axis == "x" and "x" in h.axes:
+                    h.send_x()
+                else:
+                    h.each(axis, lambda c, _: c.start())
         sent.extend(halos)
 
     def arrive(halos, axes="yxc"):
@@ -192,14 +242,18 @@
             for h in halos:
                 h.each(axis, h.unpack if axis == "c" else lambda c, _: c.wait_recv(), flip=True)
 
+    def forward(h, side):
+        h.aside(side).wait_recv()
+        h.onward(side).start()
+
     h_vel = [[Halo(0, v1.at[0], 2, 1, 2), Halo(1, v1.at[1], 1, 2, 2), Halo(2, v1.at[2], 1, 1)],
              [Halo(3, v2.at[0], 2, 1, 2), Halo(4, v2.at[1], 1, 2, 2), Halo(5, v2.at[2], 1, 1)]]
-    h_p = [[Halo(6, pin1, WX, WX, WX)], [Halo(7, pin2, WX - 1, WX - 1, WX, skip=1)]]
+    h_p = [[Halo(6, pin1, WX, WX, WX)], [Halo(7, pin2, WX - 1, WX - 1, WX, skip=1, detour=1)]]
     near = SWEEPS // 2
     h_src = [[Halo(8, src1, near, SWEEPS, SWEEPS)], [Halo(9, src2, near, SWEEPS, SWEEPS)]]
     h_far = [[Halo(14, src1, SWEEPS - near, axes="x", skip=near)], [Halo(15, src2, SWEEPS - near, axes="x", skip=near)]]
     h_solid = [Halo(10, solid, 2, WX, 2)]
-    h_rest = [Halo(13, solid, WX - 2, reach=WX, axes="x", skip=2, over=2)]
+    h_rest = [Halo(13, solid, WX - 2, reach=WX, axes="x", skip=2, over=2, detour=0)]
     h_mf = [Halo(11, mf.at[0], 1, axes="x"), Halo(12, mf.at[1], rows=1, width=0, axes="y")]
 
     for fetch in fetches[3:]:
@@ -345,6 +399,8 @@
         sweep_over(predict, [(low + 1, high - 1)], 3)
         sweep_over(balance, [(low + near, high - near)], 4)
         start(h_far[step])
+        for h in h_p[1] if step else h_rest:
+            h.pass_on(forward)
         arrive(early, "xc")
         if step == 0:
             sweep_over(voidage, [(low - 2, low), (high, high + 2)], 2)
@@ -444,6 +500,7 @@
     for h in sent:
         for axis in "xyc":
             h.each(axis, lambda c, _: c.wait_send())
+        h.pass_on(lambda h, side: h.onward(side).wait_send())
     for k in range(1, n_gy):
         outgoing(k).wait_send()
         getting(k).wait_recv()
@@ -504,6 +561,9 @@
                 pltpu.VMEM((n_gy, 1, slots), F32),
                 pltpu.VMEM((16, 4, WX * (WX - 1) // 2, 1, nz), F32),
                 pltpu.VMEM((16, 4, WX * (WX - 1) // 2, 1, nz), F32),
+                pltpu.VMEM((2, WX, by, nz), F32),
+                pltpu.SemaphoreType.DMA((2,)),
+                pltpu.SemaphoreType.DMA((2,)),
                 pltpu.SemaphoreType.DMA((16, 8)),
                 pltpu.SemaphoreType.DMA((16, 8)),
                 pltpu.SemaphoreType.DMA((2, n_gy)),

time: 47 us -> 46.3 us (0.985)
  Pallas kernels: 46.1 us -> 45.4 us
    pallas_call x1, Pallas kernels: 45.3 us -> 44.6 us  [per_device(): pl.pallas_call(kernel, name='interval', out_shape=(pltpu.VMEM(velocity.sh...]
where the time goes in v4:
time: 46.3 us; the launch traced here: 46 us
  Pallas kernels  45.4 us (98%)
  between operations  0.64 us (1%)
    pallas_call x1, Pallas kernels, per_device(): pl.pallas_call(kernel, name='interval', out_shape=(pltpu.VMEM(velocity.sh...  44.6 us

profile of v4, /device:TPU:0, one launch (start us, length us, event | category | flops | bytes accessed | tf_op | source)
XLA Modules:
  0.0 46.0 jit_solution(3461009382101106351)
XLA Ops:
  0.6 44.6 %interval.1 = (f32[3,8,16,256]{3,2,1,0:T(8,128)S(1)}, f32[8,16,256]{2,1,0:T(8,128)S(1)}, f32[3,8,512]{2,1,0:T(8,128)S(1)}) custom-call(s32[8]{0:T(128)} %bitcast.12, f32[3,8,16,256]{3,2,1,0:T(8,128)} %refs_1_.1, f32[8,16,256]{2,1,0:T(8,128)} %refs_2_.1, s32[8,512]{1,0:T(8,128)} %bitcast.10, f32[3,8,512]{2,1,0:T(8,128)} %bitcast.9, f32[8,512]{1,0:T(8,128)} %bitcast.11), custom_call_target="tpu_custom_call" | custom-call | tf_op jit(solution)/shard_map/interval/pallas_call | solution.py:538
  45.2 0.8 %deliver.1 = (f32[3,8,16,256]{3,2,1,0:T(8,128)}, f32[8,16,256]{2,1,0:T(8,128)}, f32[3,8,512]{2,1,0:T(8,128)}) custom-call(f32[3,8,16,256]{3,2,1,0:T(8,128)S(1)} %get-tuple-element.9.refs_0_, f32[8,16,256]{2,1,0:T(8,128)S(1)} %get-tuple-element.10.refs_1_, f32[3,8,512]{2,1,0:T(8,128)S(1)} %get-tuple-element.11.refs_2_), custom_call_target="tpu_custom_call" | custom-call | tf_op jit(solution)/shard_map/deliver/pallas_call | solution.py:584

commit v5 on v4

--- a/solution.py
+++ b/solution.py
@@ -309,7 +309,7 @@
     def sweep_over(act, spans, unroll):
         for first, end in spans:
             if first < end:
-                lax.fori_loop(first, end, act, 0, unroll=min(unroll, end - first))
+                lax.fori_loop(first, end, act, 0, unroll=min(2 * unroll, end - first))
 
     low, high = WX, WX + bx
 
@@ -467,7 +467,7 @@
                     pin2[x, low:high, :] = p[low:high]
             return carry
 
-        lax.fori_loop(WX, WX + bx, correct, 0, unroll=4)
+        lax.fori_loop(WX, WX + bx, correct, 0, unroll=8)
         if not final:
             for x in (WX - 1, WX + bx):
                 pin2[x, own_y, :] = held[x, own_y, :]

time: 46.3 us -> 45.4 us (0.981)
  Pallas kernels: 45.4 us -> 44.5 us
    pallas_call x1, Pallas kernels: 44.6 us -> 43.6 us  [per_device(): pl.pallas_call(kernel, name='interval', out_shape=(pltpu.VMEM(velocity.sh...]
where the time goes in v5:
time: 45.4 us; the launch traced here: 45.1 us
  Pallas kernels  44.5 us (98%)
  between operations  0.64 us (1%)
    pallas_call x1, Pallas kernels, per_device(): pl.pallas_call(kernel, name='interval', out_shape=(pltpu.VMEM(velocity.sh...  43.6 us

profile of v5, /device:TPU:0, one launch (start us, length us, event | category | flops | bytes accessed | tf_op | source)
XLA Modules:
  0.0 45.1 jit_solution(14535032562620091186)
XLA Ops:
  0.6 43.6 %interval.1 = (f32[3,8,16,256]{3,2,1,0:T(8,128)S(1)}, f32[8,16,256]{2,1,0:T(8,128)S(1)}, f32[3,8,512]{2,1,0:T(8,128)S(1)}) custom-call(s32[8]{0:T(128)} %bitcast.12, f32[3,8,16,256]{3,2,1,0:T(8,128)} %refs_1_.1, f32[8,16,256]{2,1,0:T(8,128)} %refs_2_.1, s32[8,512]{1,0:T(8,128)} %bitcast.10, f32[3,8,512]{2,1,0:T(8,128)} %bitcast.9, f32[8,512]{1,0:T(8,128)} %bitcast.11), custom_call_target="tpu_custom_call" | custom-call | tf_op jit(solution)/shard_map/interval/pallas_call | solution.py:538
  44.3 0.8 %deliver.1 = (f32[3,8,16,256]{3,2,1,0:T(8,128)}, f32[8,16,256]{2,1,0:T(8,128)}, f32[3,8,512]{2,1,0:T(8,128)}) custom-call(f32[3,8,16,256]{3,2,1,0:T(8,128)S(1)} %get-tuple-element.9.refs_0_, f32[8,16,256]{2,1,0:T(8,128)S(1)} %get-tuple-element.10.refs_1_, f32[3,8,512]{2,1,0:T(8,128)S(1)} %get-tuple-element.11.refs_2_), custom_call_target="tpu_custom_call" | custom-call | tf_op jit(solution)/shard_map/deliver/pallas_call | solution.py:584

commit v6 on v5

--- a/solution.py
+++ b/solution.py
@@ -60,6 +60,12 @@
     def beyond(corner):
         return ix + (2 * corner[0] - 1), iy + (2 * corner[1] - 1)
 
+    fetches = [(cell_hbm, cell_ref), (vol_hbm, vol_ref), (gv_hbm, gv_ref)]
+    fetches += [(vel_hbm.at[d], v1.at[d, own_x, own_y]) for d in range(3)] + [(p_hbm, pin1.at[own_x, own_y])]
+    fetches = [pltpu.make_async_copy(source, landing, fetch_sem.at[n]) for n, (source, landing) in enumerate(fetches)]
+    for fetch in fetches:
+        fetch.start()
+
     barrier = pltpu.get_barrier_semaphore()
     for k in range(1, n_gy):
         pl.semaphore_signal(barrier, inc=1, device_id=(ix, to_mate(k)), device_id_type=MESH)
@@ -80,11 +86,6 @@
             def _():
                 pl.semaphore_signal(barrier, inc=1, device_id=(origin[side], iy), device_id_type=MESH)
 
-    fetches = [(cell_hbm, cell_ref), (vol_hbm, vol_ref), (gv_hbm, gv_ref)]
-    fetches += [(vel_hbm.at[d], v1.at[d, own_x, own_y]) for d in range(3)] + [(p_hbm, pin1.at[own_x, own_y])]
-    fetches = [pltpu.make_async_copy(source, landing, fetch_sem.at[n]) for n, (source, landing) in enumerate(fetches)]
-    for fetch in fetches:
-        fetch.start()
 
     fields = [v1.at[d] for d in range(3)] + [v2.at[d] for d in range(3)] + [mf.at[d] for d in range(3)]
     fields += [pin1, pin2, src1, src2, solid]
@@ -276,12 +277,10 @@
         volume = rk[b, 1:2, :]
         values = [volume] + [volume * rk[b, 2 + d:3 + d, :] for d in range(3)]
         parts = [split(value) for value in values]
-        both = None
-        for side in (0, 1):
-            left = jnp.concatenate([jnp.where(hot_c, part[side], 0.0).astype(BF16) for part in parts], axis=0)
-            term = lax.dot_general(left, hot_z, (((1,), (1,)), ((), ())), preferred_element_type=F32)
-            both = term if both is None else both + term
-        dep[...] += both
+        left = jnp.concatenate(
+            [jnp.concatenate([jnp.where(hot_c, part[side], 0.0).astype(BF16) for side in (0, 1)], axis=1) for part in parts], axis=0)
+        dep[...] += lax.dot_general(left, jnp.concatenate([hot_z, hot_z], axis=1), (((1,), (1,)), ((), ())),
+                                    preferred_element_type=F32)
         return carry
 
     deposit(iy, 0)
@@ -392,6 +391,9 @@
             return carry
 
         early = h_vel[step] + (h_solid + h_mf if step == 0 else [])
+        if step:
+            ft[pl.ds(3 * nz, nz), :] = table(eps[own_x, own_y, :])
+            lax.fori_loop(0, n_gy, porosity, 0)
         arrive(early, "y")
         if step == 0:
             sweep_over(voidage, [(low, high)], 4)
@@ -438,8 +440,6 @@
         for sweep in range(SWEEPS):
             sweep_over(relaxing(sweep), [(low + sweep + inset, high - sweep - inset)], 4)
         if step:
-            ft[pl.ds(3 * nz, nz), :] = table(eps[own_x, own_y, :])
-            lax.fori_loop(0, n_gy, porosity, 0)
             arrive(h_p[step], "xc")
         arrive(h_src[step], "xc")
         arrive(h_far[step])

time: 45.4 us -> 45 us (level)
  no operation moved by 1% of the time
where the time goes in v6:
time: 45 us; the launch traced here: 44.7 us
  Pallas kernels  44.1 us (98%)
  between operations  0.64 us (1%)
    pallas_call x1, Pallas kernels, per_device(): pl.pallas_call(kernel, name='interval', out_shape=(pltpu.VMEM(velocity.sh...  43.3 us

profile of v6, /device:TPU:0, one launch (start us, length us, event | category | flops | bytes accessed | tf_op | source)
XLA Modules:
  0.0 44.7 jit_solution(12822947897730590564)
XLA Ops:
  0.6 43.3 %interval.1 = (f32[3,8,16,256]{3,2,1,0:T(8,128)S(1)}, f32[8,16,256]{2,1,0:T(8,128)S(1)}, f32[3,8,512]{2,1,0:T(8,128)S(1)}) custom-call(s32[8]{0:T(128)} %bitcast.12, f32[3,8,16,256]{3,2,1,0:T(8,128)} %refs_1_.1, f32[8,16,256]{2,1,0:T(8,128)} %refs_2_.1, s32[8,512]{1,0:T(8,128)} %bitcast.10, f32[3,8,512]{2,1,0:T(8,128)} %bitcast.9, f32[8,512]{1,0:T(8,128)} %bitcast.11), custom_call_target="tpu_custom_call" | custom-call | tf_op jit(solution)/shard_map/interval/pallas_call | solution.py:538
  43.9 0.8 %deliver.1 = (f32[3,8,16,256]{3,2,1,0:T(8,128)}, f32[8,16,256]{2,1,0:T(8,128)}, f32[3,8,512]{2,1,0:T(8,128)}) custom-call(f32[3,8,16,256]{3,2,1,0:T(8,128)S(1)} %get-tuple-element.9.refs_0_, f32[8,16,256]{2,1,0:T(8,128)S(1)} %get-tuple-element.10.refs_1_, f32[3,8,512]{2,1,0:T(8,128)S(1)} %get-tuple-element.11.refs_2_), custom_call_target="tpu_custom_call" | custom-call | tf_op jit(solution)/shard_map/deliver/pallas_call | solution.py:584

commit v7 on v6

--- a/solution.py
+++ b/solution.py
@@ -227,15 +227,18 @@
 
     sent = []
 
+    def send(halos, axis):
+        for h in halos:
+            if axis == "x" and "x" in h.axes:
+                h.send_x()
+            else:
+                h.each(axis, lambda c, _: c.start())
+
     def start(halos):
         for h in halos:
             h.pack()
         for axis in "cxy":
-            for h in halos:
-                if axis == "x" and "x" in h.axes:
-                    h.send_x()
-                else:
-                    h.each(axis, lambda c, _: c.start())
+            send(halos, axis)
         sent.extend(halos)
 
     def arrive(halos, axes="yxc"):
@@ -249,12 +252,12 @@
 
     h_vel = [[Halo(0, v1.at[0], 2, 1, 2), Halo(1, v1.at[1], 1, 2, 2), Halo(2, v1.at[2], 1, 1)],
              [Halo(3, v2.at[0], 2, 1, 2), Halo(4, v2.at[1], 1, 2, 2), Halo(5, v2.at[2], 1, 1)]]
-    h_p = [[Halo(6, pin1, WX, WX, WX)], [Halo(7, pin2, WX - 1, WX - 1, WX, skip=1, detour=1)]]
+    h_p = [[Halo(6, pin1, WX, WX, WX)], [Halo(7, pin2, WX - 1, WX - 1, WX, skip=1, detour=0)]]
     near = SWEEPS // 2
     h_src = [[Halo(8, src1, near, SWEEPS, SWEEPS)], [Halo(9, src2, near, SWEEPS, SWEEPS)]]
     h_far = [[Halo(14, src1, SWEEPS - near, axes="x", skip=near)], [Halo(15, src2, SWEEPS - near, axes="x", skip=near)]]
     h_solid = [Halo(10, solid, 2, WX, 2)]
-    h_rest = [Halo(13, solid, WX - 2, reach=WX, axes="x", skip=2, over=2, detour=0)]
+    h_rest = [Halo(13, solid, WX - 2, reach=WX, axes="x", skip=2, over=2)]
     h_mf = [Halo(11, mf.at[0], 1, axes="x"), Halo(12, mf.at[1], rows=1, width=0, axes="y")]
 
     for fetch in fetches[3:]:
@@ -374,14 +377,18 @@
         pin = (pin1, pin2)[step]
         src = (src1, src2)[step]
 
-        def predict(x, carry):
-            s, r, g, e = solid[x], rate[x], pull[x], eps[x]
-            for d in range(3):
-                old, mean = stencil(v.at[d], x)
-                new = old + r * (mean - old) + g * (mf[d, x] - s * old)
-                guess[d, x] = new
-                flux[d, x] = e * new
-            return carry
+        def predicting(parts):
+            def predict(x, carry):
+                s, r, g, e = solid[x], rate[x], pull[x], eps[x]
+                for d in range(parts):
+                    old, mean = stencil(v.at[d], x)
+                    new = old + r * (mean - old) + g * (mf[d, x] - s * old)
+                    if parts == 3:
+                        guess[d, x] = new
+                    flux[d, x] = e * new
+                return carry
+
+            return predict
 
         def balance(x, carry):
             f1, f2 = flux[1, x], flux[2, x]
@@ -398,16 +405,17 @@
         if step == 0:
             sweep_over(voidage, [(low, high)], 4)
             sweep_over(weights, [(low + 1, high - 1)], 3)
-        sweep_over(predict, [(low + 1, high - 1)], 3)
+        sweep_over(predicting(3), [(low + 1, high - 1)], 3)
         sweep_over(balance, [(low + near, high - near)], 4)
         start(h_far[step])
-        for h in h_p[1] if step else h_rest:
+        for h in h_p[1] if step else ():
             h.pass_on(forward)
         arrive(early, "xc")
         if step == 0:
             sweep_over(voidage, [(low - 2, low), (high, high + 2)], 2)
             sweep_over(weights, [(low - 1, low + 1), (high - 1, high + 1)], 2)
-        sweep_over(predict, [(low - 1, low + 1), (high - 1, high + 1)], 2)
+        sweep_over(predicting(1), [(low - 1, low), (high, high + 1)], 1)
+        sweep_over(predicting(3), [(low, low + 1), (high - 1, high)], 1)
         sweep_over(balance, [(low, low + near), (high - near, high)], 2)
         start(h_src[step])
         arrive(h_src[step], "y")
@@ -467,11 +475,19 @@
                     pin2[x, low:high, :] = p[low:high]
             return carry
 
-        lax.fori_loop(WX, WX + bx, correct, 0, unroll=8)
-        if not final:
+        if final:
+            sweep_over(correct, [(low, high)], bx)
+        else:
+            sweep_over(correct, [(low, low + 2), (high - 2, high)], 2)
+            for h in h_vel[step + 1]:
+                h.pack()
+            for axis in "cx":
+                send(h_vel[step + 1], axis)
+            sweep_over(correct, [(low + 2, high - 2)], bx)
+            send(h_vel[step + 1], "y")
+            sent.extend(h_vel[step + 1])
             for x in (WX - 1, WX + bx):
                 pin2[x, own_y, :] = held[x, own_y, :]
-            start(h_vel[step + 1])
             start(h_p[step + 1])
 
     for d in range(3):
@@ -561,7 +577,7 @@
                 pltpu.VMEM((n_gy, 1, slots), F32),
                 pltpu.VMEM((16, 4, WX * (WX - 1) // 2, 1, nz), F32),
                 pltpu.VMEM((16, 4, WX * (WX - 1) // 2, 1, nz), F32),
-                pltpu.VMEM((2, WX, by, nz), F32),
+                pltpu.VMEM((1, WX, by, nz), F32),
                 pltpu.SemaphoreType.DMA((2,)),
                 pltpu.SemaphoreType.DMA((2,)),
                 pltpu.SemaphoreType.DMA((16, 8)),

time: 45 us -> 44.9 us (level)
  no operation moved by 1% of the time
where the time goes in v7:
time: 44.9 us; the launch traced here: 44.7 us
  Pallas kernels  44 us (98%)
  between operations  0.64 us (1%)
    pallas_call x1, Pallas kernels, per_device(): pl.pallas_call(kernel, name='interval', out_shape=(pltpu.VMEM(velocity.sh...  43.2 us

profile of v7, /device:TPU:0, one launch (start us, length us, event | category | flops | bytes accessed | tf_op | source)
XLA Modules:
  0.0 44.7 jit_solution(2961987527283700542)
XLA Ops:
  0.6 43.2 %interval.1 = (f32[3,8,16,256]{3,2,1,0:T(8,128)S(1)}, f32[8,16,256]{2,1,0:T(8,128)S(1)}, f32[3,8,512]{2,1,0:T(8,128)S(1)}) custom-call(s32[8]{0:T(128)} %bitcast.12, f32[3,8,16,256]{3,2,1,0:T(8,128)} %refs_1_.1, f32[8,16,256]{2,1,0:T(8,128)} %refs_2_.1, s32[8,512]{1,0:T(8,128)} %bitcast.10, f32[3,8,512]{2,1,0:T(8,128)} %bitcast.9, f32[8,512]{1,0:T(8,128)} %bitcast.11), custom_call_target="tpu_custom_call" | custom-call | tf_op jit(solution)/shard_map/interval/pallas_call | solution.py:554
  43.8 0.8 %deliver.1 = (f32[3,8,16,256]{3,2,1,0:T(8,128)}, f32[8,16,256]{2,1,0:T(8,128)}, f32[3,8,512]{2,1,0:T(8,128)}) custom-call(f32[3,8,16,256]{3,2,1,0:T(8,128)S(1)} %get-tuple-element.9.refs_0_, f32[8,16,256]{2,1,0:T(8,128)S(1)} %get-tuple-element.10.refs_1_, f32[3,8,512]{2,1,0:T(8,128)S(1)} %get-tuple-element.11.refs_2_), custom_call_target="tpu_custom_call" | custom-call | tf_op jit(solution)/shard_map/deliver/pallas_call | solution.py:600

commit v8 on v7

--- a/solution.py
+++ b/solution.py
@@ -510,7 +510,7 @@
         giving(n_gy - k).start()
         return carry
 
-    lax.fori_loop(1, n_gy, gather_for, 0)
+    lax.fori_loop(1, n_gy, gather_for, 0, unroll=min(7, n_gy - 1))
     gather(iy, 0)
     rd[iy] = dk[iy]
     for h in sent:

time: 44.9 us -> 44.8 us (level)
  no operation moved by 1% of the time
where the time goes in v8:
time: 44.8 us; the launch traced here: 44.5 us
  Pallas kernels  43.9 us (98%)
  between operations  0.64 us (1%)
    pallas_call x1, Pallas kernels, per_device(): pl.pallas_call(kernel, name='interval', out_shape=(pltpu.VMEM(velocity.sh...  43.1 us

profile of v8, /device:TPU:0, one launch (start us, length us, event | category | flops | bytes accessed | tf_op | source)
XLA Modules:
  0.0 44.5 jit_solution(2177436768297930398)
XLA Ops:
  0.6 43.1 %interval.1 = (f32[3,8,16,256]{3,2,1,0:T(8,128)S(1)}, f32[8,16,256]{2,1,0:T(8,128)S(1)}, f32[3,8,512]{2,1,0:T(8,128)S(1)}) custom-call(s32[8]{0:T(128)} %bitcast.12, f32[3,8,16,256]{3,2,1,0:T(8,128)} %refs_1_.1, f32[8,16,256]{2,1,0:T(8,128)} %refs_2_.1, s32[8,512]{1,0:T(8,128)} %bitcast.10, f32[3,8,512]{2,1,0:T(8,128)} %bitcast.9, f32[8,512]{1,0:T(8,128)} %bitcast.11), custom_call_target="tpu_custom_call" | custom-call | tf_op jit(solution)/shard_map/interval/pallas_call | solution.py:554
  43.7 0.8 %deliver.1 = (f32[3,8,16,256]{3,2,1,0:T(8,128)}, f32[8,16,256]{2,1,0:T(8,128)}, f32[3,8,512]{2,1,0:T(8,128)}) custom-call(f32[3,8,16,256]{3,2,1,0:T(8,128)S(1)} %get-tuple-element.9.refs_0_, f32[8,16,256]{2,1,0:T(8,128)S(1)} %get-tuple-element.10.refs_1_, f32[3,8,512]{2,1,0:T(8,128)S(1)} %get-tuple-element.11.refs_2_), custom_call_target="tpu_custom_call" | custom-call | tf_op jit(solution)/shard_map/deliver/pallas_call | solution.py:600
